TPU v7x, 32 devices: a whole 2x2x4 slice. The times are simulated.
32 devices in a mesh: groups: 2 (over y), trades: 8 (over z, x), dates: 2 (over core).
Axes of the slice: x: 2, y: 2, z: 4, core: 2. Of those that a mesh axis runs over, the one named last changes fastest.
Arguments:
- basis_values: bfloat16 [8, 256, 256], P('dates', 'groups'), parts along dimension 1, may hold values from -6 to 6
- coefficients: bfloat16 [8192, 256], P('trades'), may hold values from -0.0625 to 0.0625
- set_map: int32 [8192], P('trades'), may hold values from 0 to 255, as said below
- trade_type: int32 [8192], P('trades'), may hold values from 0 to 15
- type_gain: float32 [8, 16], P('dates'), may hold values from 0.25 to 4
- set_lags: int32 [256], replicated, may hold values from 1 to 2
- thresholds: float32 [256], replicated, may hold values from -1 to 1
Outputs:
- coef_grad: float32 [16384, 256], P(('groups', 'trades'), 'dates'), parts along dimension 0
There are 2 independent parts, one for each index of `groups`. A program takes and returns all parts, laid end to end along the dimension named above; an argument that names none is the same for every part. Nothing has to cross between parts.
Inputs may be any that keep to these rules, and one draw needn't show every extreme that they name: `set_map`: in every aligned block of 1024 trades, exactly 128 trades fall in each group of 32 consecutive netting sets (sets g * 32 to (g + 1) * 32 - 1).
All inputs are finite; a program needn't handle non-finite values.
Results may differ from a plain program's by a relative error of at most 0.0018.
Values may be sent and summed in bfloat16 or wider, within the bound.
A program may use at most 64 MiB of HBM per device.

v0:
```python
import math

import jax
import jax.numpy as jnp
from jax import lax
from jax.sharding import PartitionSpec as P

LAG_MAX = 2


def shifted(array, axis, by):
    peers = lax.axis_size(axis)
    pairs = [(i, i + by) for i in range(peers) if 0 <= i + by < peers]
    return lax.ppermute(array, axis, pairs)


def on_device(basis_values, coefficients, set_map, trade_type, type_gain, set_lags, thresholds):
    set_count = thresholds.shape[0]
    type_count = type_gain.shape[1]
    local_dates = basis_values.shape[0]
    path_count = basis_values.shape[1]
    trade_local = coefficients.shape[0]
    loss_scale = 2.0 / math.sqrt(local_dates * lax.axis_size("dates") * path_count)
    empty_grad = jnp.zeros((trade_local, coefficients.shape[1]), jnp.float32)
    owner_count = lax.axis_size("trades")
    own_sets = set_count // owner_count
    set_owner = set_map // own_sets
    route_order = jnp.argsort(set_owner, stable=True)
    coef_sorted = jnp.take(coefficients, route_order, axis=0)
    labels = jnp.take(set_map * type_count + trade_type, route_order, axis=0)
    recv_coef = lax.all_to_all(coef_sorted, "trades", split_axis=0, concat_axis=0, tiled=True)
    recv_label = lax.all_to_all(labels, "trades", split_axis=0, concat_axis=0, tiled=True)
    first_set = lax.axis_index("trades") * own_sets
    local_set = recv_label // type_count - first_set
    own_member = (local_set[:, None] == jnp.arange(own_sets, dtype=jnp.int32)[None, :]).astype(
        jnp.bfloat16
    )
    type_onehot = (
        (recv_label % type_count)[:, None] == jnp.arange(type_count, dtype=jnp.int32)[None, :]
    ).astype(jnp.float32)
    own_gain = jnp.einsum(
        "dy,ty->dt",
        type_gain,
        type_onehot,
        precision=lax.Precision.HIGHEST,
        preferred_element_type=jnp.float32,
    )
    lag_rows = lax.dynamic_slice_in_dim(set_lags, first_set, own_sets, 0)
    limit_rows = lax.dynamic_slice_in_dim(thresholds, first_set, own_sets, 0)
    netted_dates = []
    for which_date in range(local_dates):
        raw_value = jnp.einsum(
            "pk,tk->pt", basis_values[which_date], recv_coef, preferred_element_type=jnp.float32
        )
        prices = (raw_value * own_gain[which_date][None, :]).astype(jnp.bfloat16)
        netted_dates.append(jnp.dot(prices, own_member, preferred_element_type=jnp.float32))
    netted = jnp.stack(netted_dates, axis=1)
    previous = shifted(netted[:, local_dates - LAG_MAX :, :], "dates", 1)
    padded = jnp.concatenate([previous, netted], axis=1)
    collateral = jnp.zeros_like(netted)
    for lag_value in range(1, LAG_MAX + 1):
        lag_mask = (lag_rows == lag_value).astype(jnp.float32)
        collateral = (
            collateral
            + lag_mask * padded[:, LAG_MAX - lag_value : LAG_MAX - lag_value + local_dates, :]
        )
    exposure = jnp.maximum(netted - collateral - limit_rows, 0.0)
    direct_term = exposure * loss_scale
    following = shifted(direct_term[:, :LAG_MAX, :].astype(jnp.bfloat16), "dates", -1).astype(
        jnp.float32
    )
    padded_back = jnp.concatenate([direct_term, following], axis=1)
    adjoint = direct_term
    for lag_value in range(1, LAG_MAX + 1):
        lag_mask = (lag_rows == lag_value).astype(jnp.float32)
        adjoint = adjoint - lag_mask * padded_back[:, lag_value : lag_value + local_dates, :]
    adjoint = adjoint.astype(jnp.bfloat16)
    total_grad = empty_grad
    for which_date in range(local_dates):
        spread = jnp.einsum(
            "ps,ts->pt", adjoint[:, which_date, :], own_member, preferred_element_type=jnp.float32
        )
        scaled = (spread * own_gain[which_date][None, :]).astype(jnp.bfloat16)
        total_grad = total_grad + jnp.einsum(
            "pt,pk->tk", scaled, basis_values[which_date], preferred_element_type=jnp.float32
        )
    own_grad = total_grad
    returned = lax.all_to_all(own_grad, "trades", split_axis=0, concat_axis=0, tiled=True)
    inverse = jnp.argsort(route_order, stable=True)
    total_grad = jnp.take(returned, inverse, axis=0)
    return lax.psum_scatter(total_grad, "dates", scatter_dimension=1, tiled=True)


def solution(mesh):
    return jax.shard_map(
        on_device,
        mesh=mesh,
        in_specs=(
            P("dates", "groups", None),
            P("trades", None),
            P("trades"),
            P("trades"),
            P("dates", None),
            P(),
            P(),
        ),
        out_specs=P(("groups", "trades"), "dates"),
        check_vma=False,
    )
```

profile of v0, /device:TPU:0, one launch (start us, length us, event | category | flops | bytes accessed | tf_op | source)
XLA Modules:
  0.0 108.8 jit_solution(13513787980426994334)
XLA Ops:
  6.5 0.0 copy-start
  6.5 0.8 add_select_fusion.2
  7.3 4.4 %sort.31 = (s32[1024]{0:T(1024)}, s32[1024]{0:T(1024)S(1)}) sort(s32[1024]{0:T(1024)S(1)} %get-tuple-element.17, s32[1024]{0:T(1024)S(1)} %iota.15), dimensions={0}, to_apply=%region_0.1 | sort | flops 10240 | bytes 16384 | tf_op jit(solution)/shard_map/jit(argsort)/sort | solution.py:28
  11.7 4.5 %gather_fusion.1 = s32[1024]{0:T(1024)S(1)} fusion(s32[1024]{0:T(1024)S(1)} %get-tuple-element.18, s32[1024]{0:T(1024)S(1)} %fusion.79), kind=kCustom, calls=%fused_computation.1 | custom fusion | bytes 12288 | tf_op jit(solution)/shard_map/jit(_take)/gather | solution.py:30
  16.2 0.6 broadcast_select_fusion.2
  16.8 7.3 %all-to-all-start.1 = ((s32[8,128,1]{1,2,0:T(1,128)}), s32[8,128,1]{1,2,0:T(1,128)S(1)}, u32[]{:S(2)}, u32[]{:S(2)}) async-start(s32[8,128,1]{1,2,0:T(1,128)} %bitcast.5), calls=%async_computation.1 | async-start | bytes 8192 | tf_op jit(solution)/shard_map/all_to_all | solution.py:32
  24.1 0.0 copy-done
  24.1 3.9 %gather_fusion = bf16[1024,256]{1,0:T(8,128)(2,1)S(1)} fusion(bf16[1024,256]{1,0:T(8,128)(2,1)S(1)} %copy-done, s32[1024]{0:T(1024)S(1)} %fusion.79), kind=kCustom, calls=%fused_computation | custom fusion | bytes 1052672 | tf_op jit(solution)/shard_map/jit(_take)/gather | solution.py:29
  28.0 1.0 broadcast_select_fusion.1
  29.0 0.0 copy-start.1
  29.0 1.5 %all-to-all-done.1 = s32[8,128,1]{1,2,0:T(1,128)S(1)} async-done(((s32[8,128,1]{1,2,0:T(1,128)}), s32[8,128,1]{1,2,0:T(1,128)S(1)}, u32[]{:S(2)}, u32[]{:S(2)}) %all-to-all-start.1) | async-done | bytes 4128 | tf_op jit(solution)/shard_map/all_to_all | solution.py:32
  30.6 4.6 %all-to-all-start = ((bf16[8,128,256]{2,1,0:T(8,128)(2,1)}), bf16[8,128,256]{2,1,0:T(8,128)(2,1)S(1)}, u32[]{:S(2)}, u32[]{:S(2)}) async-start(bf16[8,128,256]{2,1,0:T(8,128)(2,1)} %broadcast_select_fusion.1), calls=%async_computation | async-start | bytes 1048576 | tf_op jit(solution)/shard_map/all_to_all | solution.py:31
  35.2 0.0 copy-start.4
  35.2 0.7 copy-done.4
  35.9 0.0 copy-start.2
  35.9 0.1 dynamic_slice.7
  35.9 0.6 copy-done.2
  36.5 0.1 compare_convert_fusion.1
  36.6 0.0 copy-start.3
  36.6 0.7 copy-done.3
  37.3 0.4 convolution_bitcast_fusion
  37.8 11.4 %all-to-all-done = bf16[8,128,256]{2,1,0:T(8,128)(2,1)S(1)} async-done(((bf16[8,128,256]{2,1,0:T(8,128)(2,1)}), bf16[8,128,256]{2,1,0:T(8,128)(2,1)S(1)}, u32[]{:S(2)}, u32[]{:S(2)}) %all-to-all-start) | async-done | bytes 524320 | tf_op jit(solution)/shard_map/all_to_all | solution.py:31
  49.1 0.0 copy-done.1
  49.1 0.6 fusion.16
  49.7 0.6 fusion.15
  50.4 1.3 %collective-permute-start = (f32[128,2,32]{0,2,1:T(8,128)S(1)}, f32[128,2,32]{0,2,1:T(8,128)S(1)}, u32[]{:S(2)}, u32[]{:S(2)}) collective-permute-start(f32[128,2,32]{0,2,1:T(8,128)S(1)} %pad_maximum_fusion.4), channel_id=1, source_target_pairs={{0,1},{2,3},{4,5},{6,7},{8,9},{10,11},{12,13},{14,15},{16,17},{18,... | collective-permute-start | bytes 98312 | tf_op jit(solution)/shard_map/ppermute | solution.py:14
  51.7 0.6 fusion.13
  52.3 0.6 fusion.14
  52.9 0.0 collective-permute-done
  52.9 0.1 fusion.49
  53.0 1.3 %collective-permute-start.1 = (bf16[128,2,32]{0,2,1:T(8,128)(2,1)S(1)}, bf16[128,2,32]{0,2,1:T(8,128)(2,1)S(1)}, u32[]{:S(2)}, u32[]{:S(2)}) collective-permute-start(bf16[128,2,32]{0,2,1:T(8,128)(2,1)S(1)} %slice.158), channel_id=1, source_target_pairs={{1,0},{3,2},{5,4},{7,6},{9,8},{11,10},{13,12},{15,14},{17,16},{19,... | collective-permute-start | bytes 49160 | tf_op jit(solution)/shard_map/ppermute | solution.py:14
  54.3 1.8 %collective-permute-done.1 = bf16[128,2,32]{0,2,1:T(8,128)(2,1)S(1)} collective-permute-done((bf16[128,2,32]{0,2,1:T(8,128)(2,1)S(1)}, bf16[128,2,32]{0,2,1:T(8,128)(2,1)S(1)}, u32[]{:S(2)}, u32[]{:S(2)}) %collective-permute-start.1) | collective-permute-done | bytes 16416 | tf_op jit(solution)/shard_map/ppermute | solution.py:14
  56.1 0.1 fusion.42
  56.2 0.6 fusion.12
  56.8 0.6 convolution_add_fusion.2
  57.5 0.6 convolution_add_fusion.1
  58.1 1.6 %convolution_add_fusion = f32[1024,256]{1,0:T(8,128)} fusion(f32[1024,256]{1,0:T(8,128)S(1)} %convolution_add_fusion.1, f32[1024]{0:T(1024)S(1)} %bitcast.75, s32[1024]{0:T(1024)S(1)} %get-tuple-element.15, bf16[4,128,256]{2,1,0:T(8,128)(2,1)S(1)} %copy-done.1, bf16[128,4,32]{0,2,1:T(8,128)(2,1)S(1)} %fusion.42), kind=kOutput, calls=%fused_computation.3 | convolution fusion | flops 76054528 | bytes 2179072 | tf_op jit(solution)/shard_map/pt,pk->tk/dot_general | solution.py:84
  59.7 3.8 %all-to-all-start.2 = ((f32[8,128,256]{2,1,0:T(8,128)}), f32[8,128,256]{2,1,0:T(8,128)S(1)}, u32[]{:S(2)}, u32[]{:S(2)}) async-start(f32[8,128,256]{2,1,0:T(8,128)} %bitcast.23), calls=%async_computation.2 | async-start | bytes 2097152 | tf_op jit(solution)/shard_map/all_to_all | solution.py:88
  63.6 0.0 reduce-scatter.2.cloned.1.call-start
  63.6 4.4 %sort.32 = (s32[1024]{0:T(1024)}, s32[1024]{0:T(1024)S(1)}) sort(s32[1024]{0:T(1024)S(1)} %get-tuple-element.7, s32[1024]{0:T(1024)S(1)} %iota.16), dimensions={0}, to_apply=%region_1.2 | sort | flops 10240 | bytes 16384 | tf_op jit(solution)/shard_map/jit(argsort)/sort | solution.py:89
  68.0 21.7 %all-to-all-done.2 = f32[8,128,256]{2,1,0:T(8,128)S(1)} async-done(((f32[8,128,256]{2,1,0:T(8,128)}), f32[8,128,256]{2,1,0:T(8,128)S(1)}, u32[]{:S(2)}, u32[]{:S(2)}) %all-to-all-start.2) | async-done | bytes 1048608 | tf_op jit(solution)/shard_map/all_to_all | solution.py:88
  89.7 3.5 %gather_fusion.2 = f32[1024,256]{1,0:T(8,128)S(1)} fusion(f32[1024,256]{1,0:T(8,128)S(1)} %bitcast.68, s32[1024]{0:T(1024)S(1)} %fusion.78), kind=kCustom, calls=%fused_computation.2 | custom fusion | bytes 2101248 | tf_op jit(solution)/shard_map/jit(_take)/gather | solution.py:90
  93.1 1.2 %broadcast_select_fusion = f32[1024,256]{1,0:T(8,128)} fusion(f32[1024,256]{1,0:T(8,128)S(1)} %gather_fusion.2, pred[1024]{0:T(1024)(128)(4,1)S(1)} %compare_and_fusion.1), kind=kLoop, calls=%fused_computation.32 | loop fusion | flops 262144 | bytes 2098176 | tf_op jit(solution)/shard_map/jit(_take)/select_n | solution.py:90
  94.3 0.0 reduce-scatter.2.cloned.1.call-update
  94.3 7.6 %reduce-scatter.2.cloned.1.call-done = f32[1024,128]{1,0:T(8,128)} async-done(((f32[1024,256]{1,0:T(8,128)}), f32[1024,128]{1,0:T(8,128)}) %reduce-scatter.2.cloned.1.call-update) | async-done | bytes 524304 | tf_op jit(solution)/shard_map/reduce_scatter | solution.py:91
  (10 shorter events, 0.1 us)
Async XLA Ops:
  6.5 17.6 %copy-start = (bf16[1024,256]{1,0:T(8,128)(2,1)S(1)}, bf16[1024,256]{1,0:T(8,128)(2,1)}, u32[]{:S(2)}) copy-start(bf16[1024,256]{1,0:T(8,128)(2,1)} %param.8) | copy-start | bytes 1572868
  16.8 13.8 %all-to-all-start.1 = ((s32[8,128,1]{1,2,0:T(1,128)}), s32[8,128,1]{1,2,0:T(1,128)S(1)}, u32[]{:S(2)}, u32[]{:S(2)}) async-start(s32[8,128,1]{1,2,0:T(1,128)} %bitcast.5), calls=%async_computation.1 | async-start | bytes 8192 | tf_op jit(solution)/shard_map/all_to_all | solution.py:32
  29.0 20.1 %copy-start.1 = (bf16[4,128,256]{2,1,0:T(8,128)(2,1)S(1)}, bf16[4,128,256]{2,1,0:T(8,128)(2,1)}, u32[]{:S(2)}) copy-start(bf16[4,128,256]{2,1,0:T(8,128)(2,1)} %param.7) | copy-start | bytes 786436
  30.6 18.6 %all-to-all-start = ((bf16[8,128,256]{2,1,0:T(8,128)(2,1)}), bf16[8,128,256]{2,1,0:T(8,128)(2,1)S(1)}, u32[]{:S(2)}, u32[]{:S(2)}) async-start(bf16[8,128,256]{2,1,0:T(8,128)(2,1)} %broadcast_select_fusion.1), calls=%async_computation | async-start | bytes 1048576 | tf_op jit(solution)/shard_map/all_to_all | solution.py:31
  35.2 0.7 copy-start.4
  35.9 0.7 copy-start.2
  36.6 0.7 copy-start.3
  50.4 2.5 %collective-permute-start = (f32[128,2,32]{0,2,1:T(8,128)S(1)}, f32[128,2,32]{0,2,1:T(8,128)S(1)}, u32[]{:S(2)}, u32[]{:S(2)}) collective-permute-start(f32[128,2,32]{0,2,1:T(8,128)S(1)} %pad_maximum_fusion.4), channel_id=1, source_target_pairs={{0,1},{2,3},{4,5},{6,7},{8,9},{10,11},{12,13},{14,15},{16,17},{18,... | collective-permute-start | bytes 98312 | tf_op jit(solution)/shard_map/ppermute | solution.py:14
  53.0 3.1 %collective-permute-start.1 = (bf16[128,2,32]{0,2,1:T(8,128)(2,1)S(1)}, bf16[128,2,32]{0,2,1:T(8,128)(2,1)S(1)}, u32[]{:S(2)}, u32[]{:S(2)}) collective-permute-start(bf16[128,2,32]{0,2,1:T(8,128)(2,1)S(1)} %slice.158), channel_id=1, source_target_pairs={{1,0},{3,2},{5,4},{7,6},{9,8},{11,10},{13,12},{15,14},{17,16},{19,... | collective-permute-start | bytes 49160 | tf_op jit(solution)/shard_map/ppermute | solution.py:14
  59.7 29.9 %all-to-all-start.2 = ((f32[8,128,256]{2,1,0:T(8,128)}), f32[8,128,256]{2,1,0:T(8,128)S(1)}, u32[]{:S(2)}, u32[]{:S(2)}) async-start(f32[8,128,256]{2,1,0:T(8,128)} %bitcast.23), calls=%async_computation.2 | async-start | bytes 2097152 | tf_op jit(solution)/shard_map/all_to_all | solution.py:88
  63.6 38.4 %reduce-scatter.2.cloned.1.call-start = ((), (), s32[]{:S(2)}) async-start(), calls=%async_computation.4 | async-start | bytes 1572864 | tf_op jit(solution)/shard_map/reduce_scatter | solution.py:91
Sparse Core Ops, SparseCore 0:
  94.4 7.4 reduce-scatter.1
where the time goes:
time: 109 us
  waiting for transfers between devices  44 us (40%)
  starting transfers between devices  18.3 us (17%)
  local copies, waits for them, and re-layouts  14 us (13%)
  between operations  13.5 us (12%)
  other arithmetic  12.6 us (12%)
  matrix products  6.41 us (6%)
    all_to_all x1, waiting for transfers between devices, on_device(): lax.all_to_all(own_grad, 'trades', split_axis=0, concat_axis=0, tiled=True)  21.7 us
    all_to_all x1, waiting for transfers between devices, on_device(): lax.all_to_all(coef_sorted, 'trades', split_axis=0, concat_axis=0, tiled=...  11.4 us
    reduce_scatter x1, waiting for transfers between devices, on_device(): lax.psum_scatter(total_grad, 'dates', scatter_dimension=1, tiled=True)  7.63 us
    all_to_all x1, starting transfers between devices, on_device(): lax.all_to_all(labels, 'trades', split_axis=0, concat_axis=0, tiled=True)  7.28 us
    all_to_all x1, starting transfers between devices, on_device(): lax.all_to_all(coef_sorted, 'trades', split_axis=0, concat_axis=0, tiled=...  4.59 us
    gather x1, local copies, waits for them, and re-layouts, on_device(): labels = jnp.take(set_map * type_count + trade_type, route_order, axis=0)  4.52 us
    sort x1, other arithmetic, on_device(): route_order = jnp.argsort(set_owner, stable=True)  4.37 us
    sort x1, other arithmetic, on_device(): inverse = jnp.argsort(route_order, stable=True)  4.37 us
  transfers between devices with their start and end apart: 6, of which 5 were waited for; matrix products, arithmetic and copies ran while one was open for 10% of the time, Pallas kernels for 0%

commit v1 on v0

v1 whole, which is shorter than its diff:
```python
import functools
import math

import jax
import jax.numpy as jnp
from jax import lax
from jax.experimental import pallas as pl
from jax.experimental.pallas import tpu as pltpu
from jax.sharding import PartitionSpec as P

LAG_MAX = 2
GROUP = 8
CODE_MAX = 32767.0
NT = (((1,), (1,)), ((), ()))


def kernel(
    trade_peers, date_peers, loss_scale,
    gain_ref, basis_ref, coef_ref, set_ref, type_ref, lag_ref, limit_ref,
    out_ref,
    code_send, code_recv, unit_send, unit_recv, adj_send, adj_recv,
    member_ref, gain_cols, basis_rows, scaled_ref, half_send, half_recv,
    code_ss, code_rs, unit_ss, unit_rs, adj_ss, adj_rs, half_ss, half_rs,
):
    peers = trade_peers * date_peers
    my_trade = lax.axis_index("trades")
    my_date = lax.axis_index("dates")
    me = my_trade * date_peers + my_date
    local_dates, path_count, basis_count = basis_ref.shape
    trade_count = coef_ref.shape[0]
    set_count = limit_ref.shape[1]
    type_count = gain_ref.shape[1]
    own_paths = path_count // peers
    groups = peers // GROUP
    group_paths = GROUP * own_paths
    group_rows = local_dates * group_paths
    chunk_rows = local_dates * own_paths
    half = basis_count // date_peers

    def device(index):
        return {"trades": index // date_peers, "dates": index % date_peers}

    barrier = pltpu.get_barrier_semaphore()

    def greet(step, carry):
        pl.semaphore_signal(
            barrier, inc=1, device_id=device(lax.rem(me + step, peers)),
            device_id_type=pl.DeviceIdType.MESH,
        )
        return carry

    lax.fori_loop(1, peers, greet, 0)

    def code_copy(index, slot_here, slot_there):
        return pltpu.make_async_remote_copy(
            src_ref=code_send.at[slot_here], dst_ref=code_recv.at[slot_there],
            send_sem=code_ss.at[slot_here], recv_sem=code_rs.at[slot_there],
            device_id=device(index), device_id_type=pl.DeviceIdType.MESH,
        )

    def unit_copy(index, slot_here, slot_there):
        return pltpu.make_async_remote_copy(
            src_ref=unit_send.at[slot_here], dst_ref=unit_recv.at[slot_there],
            send_sem=unit_ss.at[slot_here], recv_sem=unit_rs.at[slot_there],
            device_id=device(index), device_id_type=pl.DeviceIdType.MESH,
        )

    def adj_copy(index, slot_there):
        return pltpu.make_async_remote_copy(
            src_ref=adj_send.at[index % date_peers], dst_ref=adj_recv.at[slot_there],
            send_sem=adj_ss.at[index], recv_sem=adj_rs.at[slot_there],
            device_id=device(index), device_id_type=pl.DeviceIdType.MESH,
        )

    types = type_ref[...]
    gains = []
    for d in range(local_dates):
        row = jnp.zeros_like(types, dtype=jnp.float32)
        for y in range(type_count):
            row = jnp.where(types == y, gain_ref[d, y], row)
        gains.append(row)
    set_ids = lax.broadcasted_iota(jnp.int32, (set_count, trade_count), 0)
    member_wide = jnp.where(set_ids == set_ref[...], 1.0, 0.0)
    member = member_wide.astype(jnp.bfloat16)

    my_group = me // GROUP

    def forward(step, carry):
        group = lax.rem(my_group + 1 + step, groups)
        rows = basis_ref[:, pl.ds(pl.multiple_of(group * group_paths, group_paths), group_paths), :]
        raw = lax.dot_general(
            rows.reshape(group_rows, basis_count), coef_ref[...], NT,
            preferred_element_type=jnp.float32,
        )
        prices = jnp.concatenate(
            [raw[d * group_paths:(d + 1) * group_paths] * gains[d] for d in range(local_dates)], axis=0
        ).astype(jnp.bfloat16)
        part = lax.dot_general(prices, member, NT, preferred_element_type=jnp.float32)
        part = part.reshape(local_dates, GROUP, own_paths, set_count)
        for i in range(GROUP):
            chunk = part[:, i].reshape(chunk_rows, set_count)
            top = jnp.maximum(jnp.max(jnp.abs(chunk), axis=0, keepdims=True), 1e-30)
            codes = jnp.round(chunk * (CODE_MAX / top)).astype(jnp.int32)
            code_send[group * GROUP + i] = codes.astype(jnp.int16)
            unit_send[group * GROUP + i] = top * (1.0 / CODE_MAX)

        @pl.when(step == 0)
        def _():
            pl.semaphore_wait(barrier, peers - 1)

        for i in range(GROUP):
            index = group * GROUP + i

            @pl.when(index != me)
            def _():
                code_copy(index, index, me).start()
                unit_copy(index, index, me).start()

        return carry

    lax.fori_loop(0, groups, forward, 0)

    code_recv[me] = code_send[me]
    unit_recv[me] = unit_send[me]
    member_ref[...] = jnp.transpose(member_wide).astype(jnp.bfloat16)
    gain_rows = jnp.concatenate(
        [jnp.broadcast_to(gains[d], (group_paths, trade_count)) for d in range(local_dates)], axis=0
    )
    gain_cols[...] = jnp.transpose(gain_rows)

    def order_rows(group, carry):
        rows = basis_ref[:, pl.ds(pl.multiple_of(group * group_paths, group_paths), group_paths), :]
        basis_rows[pl.ds(pl.multiple_of(group * group_rows, group_rows), group_rows), :] = (
            rows.reshape(group_rows, basis_count)
        )
        return carry

    lax.fori_loop(0, groups, order_rows, 0)

    def arrived(step, carry):
        source = lax.rem(me + step, peers)
        code_copy(source, source, source).wait_recv()
        unit_copy(source, source, source).wait_recv()
        return carry

    lax.fori_loop(1, peers, arrived, 0)

    def add(trade, totals):
        result = []
        for q in range(date_peers):
            source = trade * date_peers + q
            values = code_recv[source].astype(jnp.int32).astype(jnp.float32)
            result.append(totals[q] + values * unit_recv[source])
        return tuple(result)

    totals = lax.fori_loop(
        0, trade_peers, add,
        tuple(jnp.zeros((chunk_rows, set_count), jnp.float32) for _ in range(date_peers)),
    )
    netted = [
        totals[q][d * own_paths:(d + 1) * own_paths]
        for q in range(date_peers) for d in range(local_dates)
    ]
    date_count = len(netted)
    lags = lag_ref[...]
    direct = []
    for d in range(date_count):
        value = netted[d]
        for lag in range(1, LAG_MAX + 1):
            if d >= lag:
                value = value - jnp.where(lags == lag, netted[d - lag], 0.0)
        direct.append(jnp.maximum(value - limit_ref[...], 0.0) * loss_scale)
    for q in range(date_peers):
        parts = []
        for d in range(q * local_dates, (q + 1) * local_dates):
            value = direct[d]
            for lag in range(1, LAG_MAX + 1):
                if d + lag < date_count:
                    value = value - jnp.where(lags == lag, direct[d + lag], 0.0)
            parts.append(value)
        adj_send[q] = jnp.concatenate(parts, axis=0).astype(jnp.bfloat16)

    def spread_out(step, carry):
        adj_copy(lax.rem(me + peers // 2 + step, peers), me).start()
        return carry

    lax.fori_loop(0, peers // 2, spread_out, 0)

    def spread_near(step, carry):
        adj_copy(lax.rem(me + step, peers), me).start()
        return carry

    lax.fori_loop(1, peers // 2, spread_near, 0)
    adj_recv[me] = adj_send[my_date]

    def backward(step, carry):
        group = lax.rem(my_group + step, groups)
        for i in range(GROUP):
            index = group * GROUP + i

            @pl.when(index != me)
            def _():
                adj_copy(index, index).wait_recv()

        block = adj_recv[pl.ds(pl.multiple_of(group * GROUP, GROUP), GROUP)].astype(jnp.float32)
        block = block.reshape(GROUP, local_dates, own_paths, set_count)
        block = jnp.concatenate(
            [block[i, d] for d in range(local_dates) for i in range(GROUP)], axis=0
        ).astype(jnp.bfloat16)
        spread = lax.dot_general(member_ref[...], block, NT, preferred_element_type=jnp.float32)
        scaled_ref[:, pl.ds(pl.multiple_of(group * group_rows, group_rows), group_rows)] = (
            spread * gain_cols[...]
        ).astype(jnp.bfloat16)
        return carry

    lax.fori_loop(0, groups, backward, 0)

    def half_copy(step):
        q = lax.rem(my_date + step, date_peers)
        return pltpu.make_async_remote_copy(
            src_ref=half_send.at[step - 1], dst_ref=half_recv.at[step - 1],
            send_sem=half_ss.at[step - 1], recv_sem=half_rs.at[step - 1],
            device_id={"dates": q}, device_id_type=pl.DeviceIdType.MESH,
        )

    def columns(q):
        return basis_rows[:, pl.ds(pl.multiple_of(q * half, half), half)]

    for step in range(1, date_peers):
        q = lax.rem(my_date + step, date_peers)
        half_send[step - 1] = jnp.dot(scaled_ref[...], columns(q), preferred_element_type=jnp.float32)
        half_copy(step).start()
    total = jnp.dot(scaled_ref[...], columns(my_date), preferred_element_type=jnp.float32)
    for step in range(1, date_peers):
        half_copy(step).wait_recv()
        total = total + half_recv[step - 1]
    out_ref[...] = total

    def sent(step, carry):
        index = lax.rem(me + step, peers)
        code_copy(index, index, me).wait_send()
        unit_copy(index, index, me).wait_send()
        adj_copy(index, me).wait_send()
        return carry

    lax.fori_loop(1, peers, sent, 0)
    for step in range(1, date_peers):
        half_copy(step).wait_send()


def on_device(
    trade_peers, date_peers,
    basis_values, coefficients, set_map, trade_type, type_gain, set_lags, thresholds,
):
    local_dates, path_count, basis_count = basis_values.shape
    trade_count = coefficients.shape[0]
    set_count = thresholds.shape[0]
    peers = trade_peers * date_peers
    own_paths = path_count // peers
    chunk = local_dates * own_paths
    group_rows = chunk * GROUP
    half = basis_count // date_peers
    loss_scale = 2.0 / math.sqrt(local_dates * date_peers * path_count)
    vmem = pl.BlockSpec(memory_space=pltpu.VMEM)
    dma = pltpu.SemaphoreType.DMA
    return pl.pallas_call(
        functools.partial(kernel, trade_peers, date_peers, loss_scale),
        out_shape=jax.ShapeDtypeStruct((trade_count, half), jnp.float32),
        in_specs=[pl.BlockSpec(memory_space=pltpu.SMEM)] + [vmem] * 6,
        out_specs=vmem,
        scratch_shapes=[
            pltpu.VMEM((peers, chunk, set_count), jnp.int16),
            pltpu.VMEM((peers, chunk, set_count), jnp.int16),
            pltpu.VMEM((peers, 1, set_count), jnp.float32),
            pltpu.VMEM((peers, 1, set_count), jnp.float32),
            pltpu.VMEM((date_peers, chunk, set_count), jnp.bfloat16),
            pltpu.VMEM((peers, chunk, set_count), jnp.bfloat16),
            pltpu.VMEM((trade_count, set_count), jnp.bfloat16),
            pltpu.VMEM((trade_count, group_rows), jnp.float32),
            pltpu.VMEM((path_count * local_dates, basis_count), jnp.bfloat16),
            pltpu.VMEM((trade_count, path_count * local_dates), jnp.bfloat16),
            pltpu.VMEM((date_peers - 1, trade_count, half), jnp.float32),
            pltpu.VMEM((date_peers - 1, trade_count, half), jnp.float32),
            dma((peers,)), dma((peers,)), dma((peers,)), dma((peers,)),
            dma((peers,)), dma((peers,)), dma((date_peers - 1,)), dma((date_peers - 1,)),
        ],
        compiler_params=pltpu.CompilerParams(
            collective_id=0, has_side_effects=True, vmem_limit_bytes=60 * 1024 * 1024
        ),
    )(
        type_gain, basis_values, coefficients, set_map.reshape(1, -1), trade_type.reshape(1, -1),
        set_lags.reshape(1, -1), thresholds.reshape(1, -1),
    )


def solution(mesh):
    return jax.shard_map(
        functools.partial(on_device, mesh.shape["trades"], mesh.shape["dates"]),
        mesh=mesh,
        in_specs=(
            P("dates", "groups", None),
            P("trades", None),
            P("trades"),
            P("trades"),
            P("dates", None),
            P(),
            P(),
        ),
        out_specs=P(("groups", "trades"), "dates"),
        check_vma=False,
    )
```

time: 109 us -> 29.4 us (0.27)
  waiting for transfers between devices: 44 us -> 0 us
  Pallas kernels: 0 us -> 27.3 us
  starting transfers between devices: 18.3 us -> 0 us
  between operations: 13.5 us -> 0.01 us
  other arithmetic: 12.6 us -> 0 us
  local copies, waits for them, and re-layouts: 14 us -> 1.87 us
  matrix products: 6.41 us -> 0 us
    all_to_all x3 -> x0, waiting for transfers between devices: 34.6 us -> none  [the longest x1 21.7 us: on_device(): lax.all_to_all(own_grad, 'trades', split_axis=0, concat_axis=0, tiled=True)]
    pallas_call x0 -> x1, Pallas kernels: none -> 27.3 us  [on_device(): pl.pallas_call(functools.partial(kernel, trade_peers, date_peers, loss_sc...]
    all_to_all x3 -> x0, starting transfers between devices: 15.7 us -> none  [the longest x1 7.28 us: on_device(): lax.all_to_all(labels, 'trades', split_axis=0, concat_axis=0, tiled=True)]
    gather x3 -> x0, local copies, waits for them, and re-layouts: 11.9 us -> none  [the longest x1 4.52 us: on_device(): labels = jnp.take(set_map * type_count + trade_type, route_order, axis=0)]
    sort x2 -> x0, other arithmetic: 8.73 us -> none  [the longest x1 4.37 us: on_device(): route_order = jnp.argsort(set_owner, stable=True)]
    reduce_scatter x1 -> x0, waiting for transfers between devices: 7.63 us -> none  [on_device(): lax.psum_scatter(total_grad, 'dates', scatter_dimension=1, tiled=True)]
    dot_general x9 -> x0, matrix products: 6.41 us -> none  [the longest x4 3.54 us: on_device(): jnp.einsum('pt,pk->tk', scaled, basis_values[which_date], preferred_eleme...]
    select_n x4 -> x0, other arithmetic: 3.54 us -> none  [the longest x1 1.18 us: on_device(): total_grad = jnp.take(returned, inverse, axis=0)]
  transfers between devices with their start and end apart: 6 -> 0, of which waited for: 5 -> 0; matrix products, arithmetic and copies ran while one was open for 10% -> 0% of each run, Pallas kernels for 0% -> 0%
where the time goes in v1:
time: 29.4 us; the launch traced here: 29.2 us
  Pallas kernels  27.3 us (93%)
  local copies, waits for them, and re-layouts  1.87 us (6%)
    pallas_call x1, Pallas kernels, on_device(): pl.pallas_call(functools.partial(kernel, trade_peers, date_peers, loss_sc...  27.3 us
    unnamed x1, local copies, waits for them, and re-layouts  1.87 us

profile of v1, /device:TPU:0, one launch (start us, length us, event | category | flops | bytes accessed | tf_op | source)
XLA Modules:
  0.0 29.2 jit_solution(8832958239401052520)
XLA Ops:
  0.0 27.3 %shard_map.73 = f32[1024,128]{1,0:T(8,128)} custom-call(f32[4,16]{1,0:T(4,128)} %gain_ref.1, bf16[4,128,256]{2,1,0:T(8,128)(2,1)} %basis_ref.1, bf16[1024,256]{1,0:T(8,128)(2,1)} %coef_ref.1, s32[1,1024]{1,0:T(1,128)} %bitcast.4, s32[1,1024]{1,0:T(1,128)} %bitcast.5, s32[1,256]{1,0:T(1,128)} %bitcast.6, f32[1,256]{1,0:T(1,128)} %bitcast.7), custom_call_target="tpu_custom_call" | custom-call | tf_op jit(solution)/shard_map/pallas_call | solution.py:266
  27.3 1.9 %copy.9 = f32[1024,128]{1,0:T(8,128)} copy(f32[1024,128]{1,0:T(8,128)} %shard_map.73) | data formatting | bytes 1048576

commit v2 on v1

--- a/solution.py
+++ b/solution.py
@@ -16,8 +16,9 @@
 
 def kernel(
     trade_peers, date_peers, loss_scale,
-    gain_ref, basis_ref, coef_ref, set_ref, type_ref, lag_ref, limit_ref,
+    gain_in, basis_in, coef_in, set_in, type_in, lag_in, limit_in,
     out_ref,
+    gain_ref, basis_ref, coef_ref, set_ref, type_ref, lag_ref, limit_ref, load_sem,
     code_send, code_recv, unit_send, unit_recv, adj_send, adj_recv,
     member_ref, gain_cols, basis_rows, scaled_ref, half_send, half_recv,
     code_ss, code_rs, unit_ss, unit_rs, adj_ss, adj_rs, half_ss, half_rs,
@@ -49,7 +50,18 @@
         )
         return carry
 
-    lax.fori_loop(1, peers, greet, 0)
+    lax.fori_loop(1, peers, greet, 0, unroll=peers <= 16)
+    loads = [
+        pltpu.make_async_copy(source, target, load_sem.at[i])
+        for i, (source, target) in enumerate((
+            (type_in, type_ref), (gain_in, gain_ref), (set_in, set_ref), (basis_in, basis_ref),
+            (coef_in, coef_ref), (lag_in, lag_ref), (limit_in, limit_ref),
+        ))
+    ]
+    for load in loads:
+        load.start()
+    for load in loads[:3]:
+        load.wait()
 
     def code_copy(index, slot_here, slot_there):
         return pltpu.make_async_remote_copy(
@@ -73,17 +85,20 @@
         )
 
     types = type_ref[...]
+    table = gain_ref[...]
     gains = []
     for d in range(local_dates):
         row = jnp.zeros_like(types, dtype=jnp.float32)
         for y in range(type_count):
-            row = jnp.where(types == y, gain_ref[d, y], row)
+            row = jnp.where(types == y, table[d:d + 1, y:y + 1], row)
         gains.append(row)
     set_ids = lax.broadcasted_iota(jnp.int32, (set_count, trade_count), 0)
     member_wide = jnp.where(set_ids == set_ref[...], 1.0, 0.0)
     member = member_wide.astype(jnp.bfloat16)
 
     my_group = me // GROUP
+    for load in loads[3:]:
+        load.wait()
 
     def forward(step, carry):
         group = lax.rem(my_group + 1 + step, groups)
@@ -118,7 +133,7 @@
 
         return carry
 
-    lax.fori_loop(0, groups, forward, 0)
+    lax.fori_loop(0, groups, forward, 0, unroll=groups <= 2)
 
     code_recv[me] = code_send[me]
     unit_recv[me] = unit_send[me]
@@ -135,7 +150,7 @@
         )
         return carry
 
-    lax.fori_loop(0, groups, order_rows, 0)
+    lax.fori_loop(0, groups, order_rows, 0, unroll=groups <= 2)
 
     def arrived(step, carry):
         source = lax.rem(me + step, peers)
@@ -143,7 +158,7 @@
         unit_copy(source, source, source).wait_recv()
         return carry
 
-    lax.fori_loop(1, peers, arrived, 0)
+    lax.fori_loop(1, peers, arrived, 0, unroll=peers <= 16)
 
     def add(trade, totals):
         result = []
@@ -156,6 +171,7 @@
     totals = lax.fori_loop(
         0, trade_peers, add,
         tuple(jnp.zeros((chunk_rows, set_count), jnp.float32) for _ in range(date_peers)),
+        unroll=peers <= 16,
     )
     netted = [
         totals[q][d * own_paths:(d + 1) * own_paths]
@@ -181,16 +197,10 @@
         adj_send[q] = jnp.concatenate(parts, axis=0).astype(jnp.bfloat16)
 
     def spread_out(step, carry):
-        adj_copy(lax.rem(me + peers // 2 + step, peers), me).start()
-        return carry
-
-    lax.fori_loop(0, peers // 2, spread_out, 0)
-
-    def spread_near(step, carry):
         adj_copy(lax.rem(me + step, peers), me).start()
         return carry
 
-    lax.fori_loop(1, peers // 2, spread_near, 0)
+    lax.fori_loop(1, peers, spread_out, 0, unroll=peers <= 16)
     adj_recv[me] = adj_send[my_date]
 
     def backward(step, carry):
@@ -213,7 +223,7 @@
         ).astype(jnp.bfloat16)
         return carry
 
-    lax.fori_loop(0, groups, backward, 0)
+    lax.fori_loop(0, groups, backward, 0, unroll=groups <= 2)
 
     def half_copy(step):
         q = lax.rem(my_date + step, date_peers)
@@ -231,11 +241,6 @@
         half_send[step - 1] = jnp.dot(scaled_ref[...], columns(q), preferred_element_type=jnp.float32)
         half_copy(step).start()
     total = jnp.dot(scaled_ref[...], columns(my_date), preferred_element_type=jnp.float32)
-    for step in range(1, date_peers):
-        half_copy(step).wait_recv()
-        total = total + half_recv[step - 1]
-    out_ref[...] = total
-
     def sent(step, carry):
         index = lax.rem(me + step, peers)
         code_copy(index, index, me).wait_send()
@@ -243,7 +248,12 @@
         adj_copy(index, me).wait_send()
         return carry
 
-    lax.fori_loop(1, peers, sent, 0)
+    lax.fori_loop(1, peers, sent, 0, unroll=peers <= 16)
+    for step in range(1, date_peers):
+        half_copy(step).wait_recv()
+        total = total + half_recv[step - 1]
+    out_ref[...] = total
+
     for step in range(1, date_peers):
         half_copy(step).wait_send()
 
@@ -261,14 +271,23 @@
     group_rows = chunk * GROUP
     half = basis_count // date_peers
     loss_scale = 2.0 / math.sqrt(local_dates * date_peers * path_count)
+    vmem_limit = min(60, 20 + 4 * local_dates * path_count // 512) * 1024 * 1024
     vmem = pl.BlockSpec(memory_space=pltpu.VMEM)
     dma = pltpu.SemaphoreType.DMA
     return pl.pallas_call(
         functools.partial(kernel, trade_peers, date_peers, loss_scale),
         out_shape=jax.ShapeDtypeStruct((trade_count, half), jnp.float32),
-        in_specs=[pl.BlockSpec(memory_space=pltpu.SMEM)] + [vmem] * 6,
+        in_specs=[pl.BlockSpec(memory_space=pltpu.HBM)] * 7,
         out_specs=vmem,
         scratch_shapes=[
+            pltpu.VMEM(type_gain.shape, jnp.float32),
+            pltpu.VMEM(basis_values.shape, jnp.bfloat16),
+            pltpu.VMEM(coefficients.shape, jnp.bfloat16),
+            pltpu.VMEM((1, trade_count), jnp.int32),
+            pltpu.VMEM((1, trade_count), jnp.int32),
+            pltpu.VMEM((1, set_count), jnp.int32),
+            pltpu.VMEM((1, set_count), jnp.float32),
+            dma((7,)),
             pltpu.VMEM((peers, chunk, set_count), jnp.int16),
             pltpu.VMEM((peers, chunk, set_count), jnp.int16),
             pltpu.VMEM((peers, 1, set_count), jnp.float32),
@@ -285,11 +304,16 @@
             dma((peers,)), dma((peers,)), dma((date_peers - 1,)), dma((date_peers - 1,)),
         ],
         compiler_params=pltpu.CompilerParams(
-            collective_id=0, has_side_effects=True, vmem_limit_bytes=60 * 1024 * 1024
+            collective_id=0, has_side_effects=True, vmem_limit_bytes=vmem_limit
         ),
     )(
-        type_gain, basis_values, coefficients, set_map.reshape(1, -1), trade_type.reshape(1, -1),
-        set_lags.reshape(1, -1), thresholds.reshape(1, -1),
+        *[
+            pltpu.with_memory_space_constraint(x, pltpu.HBM)
+            for x in (
+                type_gain, basis_values, coefficients, set_map.reshape(1, -1),
+                trade_type.reshape(1, -1), set_lags.reshape(1, -1), thresholds.reshape(1, -1),
+            )
+        ]
     )
 
 

time: 29.4 us -> 24.1 us (0.82)
  Pallas kernels: 27.3 us -> 23.2 us
  local copies, waits for them, and re-layouts: 1.87 us -> 0.8 us
    pallas_call x1, Pallas kernels: 27.3 us -> 23.2 us  [on_device(): pl.pallas_call(functools.partial(kernel, trade_peers, date_peers, loss_sc...]
    unnamed x1, local copies, waits for them, and re-layouts: 1.87 us -> 0.8 us
where the time goes in v2:
time: 24.1 us; the launch traced here: 24 us
  Pallas kernels  23.2 us (96%)
  local copies, waits for them, and re-layouts  0.8 us (3%)
    pallas_call x1, Pallas kernels, on_device(): pl.pallas_call(functools.partial(kernel, trade_peers, date_peers, loss_sc...  23.2 us
    unnamed x1, local copies, waits for them, and re-layouts  0.8 us

profile of v2, /device:TPU:0, one launch (start us, length us, event | category | flops | bytes accessed | tf_op | source)
XLA Modules:
  0.0 24.0 jit_solution(17290179193353504983)
XLA Ops:
  0.0 23.2 %shard_map.73 = f32[1024,128]{1,0:T(8,128)S(1)} custom-call(f32[4,16]{1,0:T(4,128)} %gain_in.1, bf16[4,128,256]{2,1,0:T(8,128)(2,1)} %basis_in.1, bf16[1024,256]{1,0:T(8,128)(2,1)} %coef_in.1, s32[1,1024]{1,0:T(1,128)} %bitcast.4, s32[1,1024]{1,0:T(1,128)} %bitcast.5, s32[1,256]{1,0:T(1,128)} %bitcast.6, f32[1,256]{1,0:T(1,128)} %bitcast.7), custom_call_target="tpu_custom_call" | custom-call | tf_op jit(solution)/shard_map/pallas_call | solution.py:277
  23.2 0.8 %copy.9 = f32[1024,128]{1,0:T(8,128)} copy(f32[1024,128]{1,0:T(8,128)S(1)} %shard_map.73) | data formatting | bytes 1048576

commit v3 on v2

--- a/solution.py
+++ b/solution.py
@@ -10,6 +10,7 @@
 
 LAG_MAX = 2
 GROUP = 8
+PIECES = 2
 CODE_MAX = 32767.0
 NT = (((1,), (1,)), ((), ()))
 
@@ -119,21 +120,18 @@
             code_send[group * GROUP + i] = codes.astype(jnp.int16)
             unit_send[group * GROUP + i] = top * (1.0 / CODE_MAX)
 
-        @pl.when(step == 0)
-        def _():
-            pl.semaphore_wait(barrier, peers - 1)
-
-        for i in range(GROUP):
-            index = group * GROUP + i
-
-            @pl.when(index != me)
-            def _():
-                code_copy(index, index, me).start()
-                unit_copy(index, index, me).start()
-
         return carry
 
     lax.fori_loop(0, groups, forward, 0, unroll=groups <= 2)
+    pl.semaphore_wait(barrier, peers - 1)
+
+    def deal(step, carry):
+        index = lax.rem(me + step, peers)
+        code_copy(index, index, me).start()
+        unit_copy(index, index, me).start()
+        return carry
+
+    lax.fori_loop(1, peers, deal, 0, unroll=peers <= 16)
 
     code_recv[me] = code_send[me]
     unit_recv[me] = unit_send[me]
@@ -225,11 +223,14 @@
 
     lax.fori_loop(0, groups, backward, 0, unroll=groups <= 2)
 
-    def half_copy(step):
+    piece_rows = trade_count // PIECES
+
+    def half_copy(step, piece):
+        rows = pl.ds(piece * piece_rows, piece_rows)
         q = lax.rem(my_date + step, date_peers)
         return pltpu.make_async_remote_copy(
-            src_ref=half_send.at[step - 1], dst_ref=half_recv.at[step - 1],
-            send_sem=half_ss.at[step - 1], recv_sem=half_rs.at[step - 1],
+            src_ref=half_send.at[step - 1, rows], dst_ref=half_recv.at[step - 1, rows],
+            send_sem=half_ss.at[step - 1, piece], recv_sem=half_rs.at[step - 1, piece],
             device_id={"dates": q}, device_id_type=pl.DeviceIdType.MESH,
         )
 
@@ -238,9 +239,14 @@
 
     for step in range(1, date_peers):
         q = lax.rem(my_date + step, date_peers)
-        half_send[step - 1] = jnp.dot(scaled_ref[...], columns(q), preferred_element_type=jnp.float32)
-        half_copy(step).start()
-    total = jnp.dot(scaled_ref[...], columns(my_date), preferred_element_type=jnp.float32)
+        for piece in range(PIECES):
+            rows = pl.ds(piece * piece_rows, piece_rows)
+            half_send[step - 1, rows] = jnp.dot(
+                scaled_ref[rows], columns(q), preferred_element_type=jnp.float32
+            )
+            half_copy(step, piece).start()
+    out_ref[...] = jnp.dot(scaled_ref[...], columns(my_date), preferred_element_type=jnp.float32)
+
     def sent(step, carry):
         index = lax.rem(me + step, peers)
         code_copy(index, index, me).wait_send()
@@ -250,12 +256,14 @@
 
     lax.fori_loop(1, peers, sent, 0, unroll=peers <= 16)
     for step in range(1, date_peers):
-        half_copy(step).wait_recv()
-        total = total + half_recv[step - 1]
-    out_ref[...] = total
+        for piece in range(PIECES):
+            rows = pl.ds(piece * piece_rows, piece_rows)
+            half_copy(step, piece).wait_recv()
+            out_ref[rows] += half_recv[step - 1, rows]
 
     for step in range(1, date_peers):
-        half_copy(step).wait_send()
+        for piece in range(PIECES):
+            half_copy(step, piece).wait_send()
 
 
 def on_device(
@@ -301,7 +309,7 @@
             pltpu.VMEM((date_peers - 1, trade_count, half), jnp.float32),
             pltpu.VMEM((date_peers - 1, trade_count, half), jnp.float32),
             dma((peers,)), dma((peers,)), dma((peers,)), dma((peers,)),
-            dma((peers,)), dma((peers,)), dma((date_peers - 1,)), dma((date_peers - 1,)),
+            dma((peers,)), dma((peers,)), dma((date_peers - 1, PIECES)), dma((date_peers - 1, PIECES)),
         ],
         compiler_params=pltpu.CompilerParams(
             collective_id=0, has_side_effects=True, vmem_limit_bytes=vmem_limit

time: 24.1 us -> 23.1 us (0.959)
  Pallas kernels: 23.2 us -> 22 us
    pallas_call x1, Pallas kernels: 23.2 us -> 22 us  [on_device(): pl.pallas_call(functools.partial(kernel, trade_peers, date_peers, loss_sc...]
where the time goes in v3:
time: 23.1 us; the launch traced here: 22.8 us
  Pallas kernels  22 us (95%)
  local copies, waits for them, and re-layouts  0.8 us (3%)
    pallas_call x1, Pallas kernels, on_device(): pl.pallas_call(functools.partial(kernel, trade_peers, date_peers, loss_sc...  22 us
    unnamed x1, local copies, waits for them, and re-layouts  0.8 us

profile of v3, /device:TPU:0, one launch (start us, length us, event | category | flops | bytes accessed | tf_op | source)
XLA Modules:
  0.0 22.8 jit_solution(7018437515823641670)
XLA Ops:
  0.0 22.0 %shard_map.73 = f32[1024,128]{1,0:T(8,128)S(1)} custom-call(f32[4,16]{1,0:T(4,128)} %gain_in.1, bf16[4,128,256]{2,1,0:T(8,128)(2,1)} %basis_in.1, bf16[1024,256]{1,0:T(8,128)(2,1)} %coef_in.1, s32[1,1024]{1,0:T(1,128)} %bitcast.4, s32[1,1024]{1,0:T(1,128)} %bitcast.5, s32[1,256]{1,0:T(1,128)} %bitcast.6, f32[1,256]{1,0:T(1,128)} %bitcast.7), custom_call_target="tpu_custom_call" | custom-call | tf_op jit(solution)/shard_map/pallas_call | solution.py:285
  22.0 0.8 %copy.9 = f32[1024,128]{1,0:T(8,128)} copy(f32[1024,128]{1,0:T(8,128)S(1)} %shard_map.73) | data formatting | bytes 1048576
